TPU v7x, 512 devices: a whole 4x4x16 slice. The times are simulated.
512 devices in a mesh: seq: 16 (over x, y_lo, core), head: 32 (over z, y_hi).
Axes of the slice: x: 4, y: 4 (y_hi: 2, y_lo: 2; y = y_hi * 2 + y_lo), z: 16, core: 2. Of those that a mesh axis runs over, the one named last changes fastest.
Arguments:
- queries: bfloat16 [65536, 4096], P(('seq', 'head')), may hold values from -56 to 56
- key_states: bfloat16 [65536, 1024], P(('seq', 'head')), may hold values from -6 to 6
- value_states: bfloat16 [65536, 1024], P(('seq', 'head')), may hold values from -6 to 6
- key_picks: int32 [128, 3], replicated, may hold values from 0 to 127, as said below
- positions: int32 [65536], P(('seq', 'head')), may hold values from 0 to 131070, as said below
Outputs:
- attended: bfloat16 [65536, 4096], P(('seq', 'head'))
Inputs may be any that keep to these rules, and one draw needn't show every extreme that they name: `positions`: strictly increasing, the first is 0 and the last is 131070. `key_picks`: the 3 entries of a row are distinct. Entries at or above the row's own block number occur only where fewer than 3 earlier blocks may be picked, name blocks from the end of the sequence, and are dropped. Groups are runs of 8 blocks; of the blocks of one group, at most 3 are picked by query blocks of later groups, and some group has exactly 3 such blocks.
All inputs are finite; a program needn't handle non-finite values.
Results may differ from a plain program's by a relative error of at most 0.02.
Values may be sent and summed in bfloat16 or wider, within the bound.
A program may use at most 64 MiB of HBM per device.

v0:
```python
import math

import jax
import jax.numpy as jnp
from jax import lax
from jax.sharding import PartitionSpec as P

HD = 128
BLOCK = 512


lowest = -1e30


def frequency_table(columns):
    inverse = 1.0 / 500000.0 ** (jnp.arange(0, columns, 2, dtype=jnp.float32) / columns)
    wavelength = 2.0 * math.pi / inverse
    smooth = (8192.0 / wavelength - 1.0) / 3.0
    blended = (1.0 - smooth) * inverse / 8.0 + smooth * inverse
    return jnp.where(
        wavelength < 2048.0, inverse, jnp.where(wavelength > 8192.0, inverse / 8.0, blended)
    )


def rotate(vectors, places):
    columns = vectors.shape[-1]
    halfway = columns // 2
    angles = places.astype(jnp.float32)[:, None] * frequency_table(columns)[None, :]
    cosine = jnp.cos(angles)[:, None, :]
    sine_of = jnp.sin(angles)[:, None, :]
    leading = vectors[..., :halfway]
    trailing = vectors[..., halfway:]
    return jnp.concatenate(
        [leading * cosine - trailing * sine_of, trailing * cosine + leading * sine_of], axis=-1
    )


def block_partial(query_block, key_block, value_block, allowed):
    scaling = 1.0 / math.sqrt(query_block.shape[-1])
    scores = (
        jnp.einsum("qkgd,skd->kgqs", query_block, key_block, preferred_element_type=jnp.float32)
        * scaling
    )
    if allowed is not None:
        scores = jnp.where(allowed, scores, lowest)
    highest = jnp.max(scores, axis=-1)
    weights = jnp.exp(scores - highest[..., None])
    summed = jnp.sum(weights, axis=-1)
    product = jnp.einsum(
        "kgqs,skd->kgqd",
        weights.astype(jnp.bfloat16),
        value_block,
        preferred_element_type=jnp.float32,
    )
    return (highest, summed, product)


def combine_stats(former, latter):
    highest = jnp.maximum(former[0], latter[0])
    former_scale = jnp.exp(former[0] - highest)
    latter_scale = jnp.exp(latter[0] - highest)
    return (
        highest,
        former[1] * former_scale + latter[1] * latter_scale,
        former[2] * former_scale[..., None] + latter[2] * latter_scale[..., None],
    )


def local(queries, key_states, value_states, key_picks, positions):
    local_rows = queries.shape[0]
    head_devices = lax.axis_size("head")
    query_heads = queries.shape[1] // HD
    shared_heads = key_states.shape[1] // HD
    repeats = max(1, head_devices // shared_heads)
    turned_queries = (
        rotate(queries.astype(jnp.float32).reshape(local_rows, query_heads, HD), positions)
        .astype(jnp.bfloat16)
        .reshape(local_rows, query_heads * HD)
    )
    turned_keys = rotate(
        key_states.astype(jnp.float32).reshape(local_rows, shared_heads, HD), positions
    ).astype(jnp.bfloat16)
    spread_keys = jnp.repeat(turned_keys, repeats, axis=1).reshape(
        local_rows, shared_heads * repeats * HD
    )
    spread_values = jnp.repeat(
        value_states.reshape(local_rows, shared_heads, HD), repeats, axis=1
    ).reshape(local_rows, shared_heads * repeats * HD)
    group_queries, group_keys, group_values = (
        lax.all_to_all(turned_queries, "head", split_axis=1, concat_axis=0, tiled=True),
        lax.all_to_all(spread_keys, "head", split_axis=1, concat_axis=0, tiled=True),
        lax.all_to_all(spread_values, "head", split_axis=1, concat_axis=0, tiled=True),
    )
    group_rows = group_queries.shape[0]
    block_count = group_rows // BLOCK
    head_local = group_queries.shape[1] // HD
    shared_local = group_keys.shape[1] // HD
    sharing = head_local // shared_local
    query_blocks = group_queries.reshape(block_count, BLOCK, shared_local, sharing, HD)
    key_blocks = group_keys.reshape(block_count, BLOCK, shared_local * HD)
    value_blocks = group_values.reshape(block_count, BLOCK, shared_local * HD)
    group_index = lax.axis_index("seq")
    first_block = group_index * block_count
    own_picks = lax.dynamic_slice_in_dim(key_picks, first_block, block_count, 0)
    pick_count = key_picks.shape[1]
    all_blocks = key_picks.shape[0]
    public = min(pick_count, block_count)
    block_ids = jnp.arange(all_blocks, dtype=jnp.int32)
    steps_in = jnp.arange(BLOCK, dtype=jnp.int32)
    causal = steps_in[:, None] >= steps_in[None, :]
    nothing = (
        jnp.full((shared_local, sharing, BLOCK), lowest, jnp.float32),
        jnp.zeros((shared_local, sharing, BLOCK), jnp.float32),
        jnp.zeros((shared_local, sharing, BLOCK, HD), jnp.float32),
    )

    def unpack(flat_rows):
        return flat_rows.reshape(BLOCK, shared_local, HD)

    def guarded(in_use, query_block, key_flat, value_flat):
        return lax.cond(
            in_use,
            lambda: block_partial(query_block, unpack(key_flat), unpack(value_flat), None),
            lambda: nothing,
        )

    def own_block(block_index):
        query_block = query_blocks[block_index]
        running = block_partial(
            query_block, unpack(key_blocks[block_index]), unpack(value_blocks[block_index]), causal
        )
        for pick_slot in range(pick_count):
            target = own_picks[block_index, pick_slot]
            in_use = (target >= first_block) & (target < first_block + block_index)
            located = jnp.clip(target - first_block, 0, block_count - 1)
            running = combine_stats(
                running, guarded(in_use, query_block, key_blocks[located], value_blocks[located])
            )
        return running

    partial_stats = lax.map(own_block, jnp.arange(block_count, dtype=jnp.int32))
    flat_keys = key_blocks.reshape(block_count, -1)
    flat_values = value_blocks.reshape(block_count, -1)
    slot_ids = jnp.arange(public, dtype=jnp.int32)
    block_group = block_ids // block_count
    picked_later = (key_picks[:, :, None] == block_ids[None, None, :]) & (
        block_group[:, None, None] > block_group[None, None, :]
    )
    is_public = jnp.any(picked_later, axis=(0, 1))
    slot_rank = (
        jnp.cumsum(is_public.reshape(-1, block_count).astype(jnp.int32), axis=1) - 1
    ).reshape(-1)
    own_public = lax.dynamic_slice_in_dim(is_public, first_block, block_count, 0)
    own_rank = lax.dynamic_slice_in_dim(slot_rank, first_block, block_count, 0)
    chooser = (own_public[None, :] & (own_rank[None, :] == slot_ids[:, None])).astype(jnp.bfloat16)
    outgoing_keys = (
        jnp.einsum("pb,bx->px", chooser, flat_keys, preferred_element_type=jnp.float32)
        .astype(jnp.bfloat16)
        .reshape(public, BLOCK, -1)
    )
    outgoing_values = (
        jnp.einsum("pb,bx->px", chooser, flat_values, preferred_element_type=jnp.float32)
        .astype(jnp.bfloat16)
        .reshape(public, BLOCK, -1)
    )
    key_rows = lax.all_gather(outgoing_keys, "seq", axis=0, tiled=True)
    value_rows = lax.all_gather(outgoing_values, "seq", axis=0, tiled=True)
    held = key_rows.shape[0]

    def far_block(bundle):
        block_index, highest, summed, product = bundle
        query_block = query_blocks[block_index]
        running = (highest, summed, product)
        for pick_slot in range(pick_count):
            target = own_picks[block_index, pick_slot]
            located = target // block_count * public + slot_rank[target]
            in_use = (target < first_block) & (located >= 0) & (located < held)
            clipped = jnp.clip(located, 0, held - 1)
            running = combine_stats(
                running, guarded(in_use, query_block, key_rows[clipped], value_rows[clipped])
            )
        return running

    partial_stats = lax.map(
        far_block, (jnp.arange(block_count, dtype=jnp.int32),) + tuple(partial_stats)
    )
    highest, summed, product = partial_stats
    attended = product / summed[..., None]
    attended = (
        jnp.transpose(attended, (0, 3, 1, 2, 4))
        .reshape(group_rows, head_local * HD)
        .astype(jnp.bfloat16)
    )
    return lax.all_to_all(attended, "head", split_axis=0, concat_axis=1, tiled=True)


def solution(mesh):
    in_specs = (
        P(("seq", "head"), None),
        P(("seq", "head"), None),
        P(("seq", "head"), None),
        P(),
        P(("seq", "head")),
    )
    out_specs = P(("seq", "head"), None)
    return jax.shard_map(local, mesh=mesh, in_specs=in_specs, out_specs=out_specs, check_vma=False)
```

profile of v0, /device:TPU:54, one launch (start us, length us, event | category | flops | bytes accessed | tf_op | source)
XLA Modules:
  0.0 665.0 jit_solution(10460114629597015019)
XLA Ops:
  10.4 17.8 %all-to-all-start = ((bf16[128,32,128]{2,0,1:T(8,128)(2,1)}), bf16[128,32,128]{2,0,1:T(8,128)(2,1)S(1)}, u32[]{:S(2)}, u32[]{:S(2)}) async-start(bf16[128,32,128]{2,0,1:T(8,128)(2,1)} %bitcast.73), calls=%async_computation | async-start | bytes 2097152 | tf_op jit(solution)/shard_map/all_to_all | solution.py:91
  29.0 53.5 %all-to-all-done = bf16[128,32,128]{2,0,1:T(8,128)(2,1)S(1)} async-done(((bf16[128,32,128]{2,0,1:T(8,128)(2,1)}), bf16[128,32,128]{2,0,1:T(8,128)(2,1)S(1)}, u32[]{:S(2)}, u32[]{:S(2)}) %all-to-all-start) | async-done | bytes 1048608 | tf_op jit(solution)/shard_map/all_to_all | solution.py:91
  85.5 6.1 all-to-all-start.2
  96.9 48.9 %all-to-all-done.2 = bf16[128,32,128]{2,0,1:T(8,128)(2,1)S(1)} async-done(((bf16[128,32,128]{2,0,1:T(8,128)(2,1)}), bf16[128,32,128]{2,0,1:T(8,128)(2,1)S(1)}, u32[]{:S(2)}, u32[]{:S(2)}) %all-to-all-start.2) | async-done | bytes 1048608 | tf_op jit(solution)/shard_map/all_to_all | solution.py:92
  145.8 5.9 all-to-all-start.1
  153.8 52.2 %all-to-all-done.1 = bf16[128,32,128]{2,0,1:T(8,128)(2,1)} async-done(((bf16[128,32,128]{2,0,1:T(8,128)(2,1)}), bf16[128,32,128]{2,0,1:T(8,128)(2,1)}, u32[]{:S(2)}, u32[]{:S(2)}) %all-to-all-start.1) | async-done | bytes 1048608 | tf_op jit(solution)/shard_map/all_to_all | solution.py:90
  207.5 115.6 %while.31 = (s32[]{:T(128)}, f32[8,1,1,512]{3,2,1,0:T(1,128)S(1)}, f32[8,1,1,512]{3,2,1,0:T(1,128)S(1)}, f32[8,1,1,512,128]{4,3,2,1,0:T(8,128)}, s32[8]{0:T(128)...) while((s32[]{:T(128)}, f32[8,1,1,512]{3,2,1,0:T(1,128)S(1)}, ...), condition=%wide.region_15.16_spmd.clone, body=%wide.region_0.15_spmd.clone.sunk | while | flops 544282112 | bytes 16338561 | solution.py:141
  323.2 272.2 %while.30 = (s32[]{:T(128)}, f32[8,1,1,512]{3,0,1,2:T(8,128)S(1)}, f32[8,1,1,512,128]{4,3,2,1,0:T(8,128)S(1)}, f32[8,1,1,512]{3,2,1,0:T(1,128)S(1)}, f32[8,1,1,5...) while((s32[]{:T(128)}, f32[8,1,1,512]{3,0,1,2:T(8,128)S(1)}, ...), condition=%wide.region_31.32_spmd, body=%wide.region_18.31_spmd.sunk | while | flops 407967776 | bytes 13049106 | solution.py:184
  336.9 4.0 conditional.15
  344.1 3.9 conditional.16
  371.0 3.9 conditional.15
  378.1 3.9 conditional.16
  405.0 3.9 conditional.15
  412.1 3.9 conditional.16
  439.0 3.9 conditional.15
  446.2 3.9 conditional.16
  473.0 3.9 conditional.15
  480.2 3.9 conditional.16
  507.1 3.9 conditional.15
  514.2 3.9 conditional.16
  541.1 3.9 conditional.15
  548.2 3.9 conditional.16
  575.1 3.9 conditional.15
  596.2 60.0 %all_to_all.61 = bf16[32,128,128]{2,1,0:T(8,128)(2,1)S(1)} all-to-all(bf16[32,128,128]{2,1,0:T(8,128)(2,1)S(1)} %bitcast.438), channel_id=1, replica_groups=mesh['seq'=16,'head'=32] {'head'}, dimensions={0} | all-to-all | bytes 2097152 | tf_op jit(solution)/shard_map/all_to_all | solution.py:194
  (352 shorter events, 265.2 us)
Async XLA Ops:
  6.5 77.6 %copy-start = (bf16[128,1024]{1,0:T(8,128)(2,1)S(1)}, bf16[128,1024]{1,0:T(8,128)(2,1)}, u32[]{:S(2)}) copy-start(bf16[128,1024]{1,0:T(8,128)(2,1)} %param.23) | copy-start | bytes 786436
  9.1 19.2 %copy-start.2 = (s32[128,3]{0,1:T(4,128)S(1)}, s32[128,3]{0,1:T(4,128)}, u32[]{:S(2)}) copy-start(s32[128,3]{0,1:T(4,128)} %param.24) | copy-start | bytes 4612
  10.4 72.0 %all-to-all-start = ((bf16[128,32,128]{2,0,1:T(8,128)(2,1)}), bf16[128,32,128]{2,0,1:T(8,128)(2,1)S(1)}, u32[]{:S(2)}, u32[]{:S(2)}) async-start(bf16[128,32,128]{2,0,1:T(8,128)(2,1)} %bitcast.73), calls=%async_computation | async-start | bytes 2097152 | tf_op jit(solution)/shard_map/all_to_all | solution.py:91
  28.1 294.9 %all-gather.3.cloned.1.call-start = ((), (), s32[]{:S(2)}) async-start(), calls=%async_computation.4 | async-start | bytes 6684672 | tf_op jit(solution)/shard_map/all_gather | solution.py:166
  84.1 7.4 %copy-start.1 = (bf16[128,4096]{1,0:T(8,128)(2,1)S(1)}, bf16[128,4096]{1,0:T(8,128)(2,1)}, u32[]{:S(2)}) copy-start(bf16[128,4096]{1,0:T(8,128)(2,1)} %param.21) | copy-start | bytes 3145732
  85.5 60.3 %all-to-all-start.2 = ((bf16[128,32,128]{2,0,1:T(8,128)(2,1)}), bf16[128,32,128]{2,0,1:T(8,128)(2,1)S(1)}, u32[]{:S(2)}, u32[]{:S(2)}) async-start(bf16[128,32,128]{2,0,1:T(8,128)(2,1)} %bitcast.78), calls=%async_computation.2 | async-start | bytes 2097152 | tf_op jit(solution)/shard_map/all_to_all | solution.py:92
  145.8 60.2 %all-to-all-start.1 = ((bf16[128,32,128]{2,0,1:T(8,128)(2,1)}), bf16[128,32,128]{2,0,1:T(8,128)(2,1)}, u32[]{:S(2)}, u32[]{:S(2)}) async-start(bf16[128,32,128]{2,0,1:T(8,128)(2,1)} %pad_maximum_fusion), calls=%async_computation.1 | async-start | bytes 2097152 | tf_op jit(solution)/shard_map/all_to_all | solution.py:90
  151.7 171.4 %all-gather.5.cloned.1.call-start = ((), (), s32[]{:S(2)}) async-start(), calls=%async_computation.5 | async-start | bytes 6684672 | tf_op jit(solution)/shard_map/all_gather | solution.py:167
Sparse Core Ops, SparseCore 0:
  84.3 50.0 all-gather.2
  154.7 55.9 all-gather.4
where the time goes:
time: 671 us; the launch traced here: 665 us
  loops' own time  190 us (28%)
  waiting for transfers between devices  155 us (23%)
  matrix products  94 us (14%)
  local copies, waits for them, and re-layouts  64 us (10%)
  blocking collectives  60 us (9%)
  other arithmetic  58.2 us (9%)
  starting transfers between devices  30 us (4%)
  between operations  13.7 us (2%)
    another operation x1, loops' own time, local(): lax.map(far_block, (jnp.arange(block_count, dtype=jnp.int32),) + tuple(pa...  139 us
    all_to_all x1, blocking collectives, local(): lax.all_to_all(attended, 'head', split_axis=0, concat_axis=1, tiled=True)  60 us
    all_to_all x1, waiting for transfers between devices, local(): lax.all_to_all(spread_keys, 'head', split_axis=1, concat_axis=0, tiled=True)  53.5 us
    dot_general x32, matrix products, block_partial(): jnp.einsum('qkgd,skd->kgqs', query_block, key_block, preferred_element_ty...  52.6 us
    all_to_all x1, waiting for transfers between devices, local(): lax.all_to_all(turned_queries, 'head', split_axis=1, concat_axis=0, tiled...  52.2 us
    another operation x1, loops' own time, local(): partial_stats = lax.map(own_block, jnp.arange(block_count, dtype=jnp.int32))  50.8 us
    all_to_all x1, waiting for transfers between devices, local(): lax.all_to_all(spread_values, 'head', split_axis=1, concat_axis=0, tiled=...  48.9 us
    dot_general x32, matrix products, block_partial(): jnp.einsum('kgqs,skd->kgqd', weights.astype(jnp.bfloat16), value_block, p...  40.6 us
  transfers between devices with their start and end apart: 5, of which 3 were waited for; matrix products, arithmetic and copies ran while one was open for 11% of the time, Pallas kernels for 0%

commit v1 on v0

v1 whole, which is shorter than its diff:
```python
import math

import jax
import jax.numpy as jnp
from jax import lax
from jax.experimental import pallas as pl
from jax.experimental.pallas import tpu as pltpu
from jax.sharding import PartitionSpec as P

HD = 128
BLOCK = 512
SHARE = 4
ROWS = BLOCK // SHARE
LOWEST = -1e30
SCALE = 1.0 / math.sqrt(HD)
LOG2E = math.log2(math.e)


def frequency_table(columns):
    inverse = 1.0 / 500000.0 ** (jnp.arange(0, columns, 2, dtype=jnp.float32) / columns)
    wavelength = 2.0 * math.pi / inverse
    smooth = (8192.0 / wavelength - 1.0) / 3.0
    blended = (1.0 - smooth) * inverse / 8.0 + smooth * inverse
    return jnp.where(
        wavelength < 2048.0, inverse, jnp.where(wavelength > 8192.0, inverse / 8.0, blended)
    )


def rope_kernel(heads, cos_ref, sin_ref, x_ref, o_ref):
    cosine = cos_ref[...]
    sine = sin_ref[...]
    for h in range(heads):
        x = x_ref[:, h * HD : (h + 1) * HD].astype(jnp.float32)
        turned = x * cosine + pltpu.roll(x, HD // 2, 1) * sine
        o_ref[:, h * HD : (h + 1) * HD] = turned.astype(jnp.bfloat16)


def kv_kernel(heads, cos_ref, sin_ref, k_ref, v_ref, o_ref):
    cosine = cos_ref[...]
    sine = sin_ref[...]
    for h in range(heads):
        x = k_ref[:, h * HD : (h + 1) * HD].astype(jnp.float32)
        turned = x * cosine + pltpu.roll(x, HD // 2, 1) * sine
        o_ref[h, :, :HD] = turned.astype(jnp.bfloat16)
        o_ref[h, :, HD:] = v_ref[:, h * HD : (h + 1) * HD]


def stacked_queries(q_ref):
    return jnp.concatenate([q_ref[:, h * HD : (h + 1) * HD] for h in range(SHARE)], axis=0)


def attend(q, kv, mask, m, l, acc):
    s = lax.dot_general(
        q, kv[:, :HD], (((1,), (1,)), ((), ())), preferred_element_type=jnp.float32
    ) * (SCALE * LOG2E)
    if mask is not None:
        s = jnp.where(mask, s, LOWEST)
    top = jnp.max(s, axis=1, keepdims=True)
    if m is not None:
        top = jnp.maximum(m, top)
    p = jnp.exp2(s - top)
    total = jnp.sum(p, axis=1, keepdims=True)
    product = jnp.dot(p.astype(jnp.bfloat16), kv[:, HD:], preferred_element_type=jnp.float32)
    if m is not None:
        keep = jnp.exp2(m - top)
        total = total + l * keep
        product = product + acc * keep
    return top, total, product


def near_kernel(table_ref, rank_ref, q_ref, own_ref, acc_ref, m_ref, l_ref):
    b = pl.program_id(0)
    q = stacked_queries(q_ref)
    row = lax.broadcasted_iota(jnp.int32, (SHARE * ROWS, BLOCK), 0) % ROWS + rank_ref[0] * ROWS
    col = lax.broadcasted_iota(jnp.int32, (SHARE * ROWS, BLOCK), 1)
    m, l, acc = attend(q, own_ref[:, b].reshape(BLOCK, 2 * HD), row >= col, None, None, None)
    m_ref[0] = m
    l_ref[0] = l
    acc_ref[0] = acc
    for slot in range(3):
        target = table_ref[b * 3 + slot]

        @pl.when(target >= 0)
        def _():
            kv = own_ref[:, jnp.maximum(target, 0)].reshape(BLOCK, 2 * HD)
            m, l, acc = attend(q, kv, None, m_ref[0], l_ref[0], acc_ref[0])
            m_ref[0] = m
            l_ref[0] = l
            acc_ref[0] = acc


def far_kernel(
    table_ref, q_ref, kv0_ref, kv1_ref, kv2_ref, acc_in, m_in, l_in, o_ref, acc_ref, m_ref, l_ref
):
    b = pl.program_id(0)
    q = stacked_queries(q_ref)
    m_ref[...] = m_in[0]
    l_ref[...] = l_in[0]
    acc_ref[...] = acc_in[0]
    for slot, kv_ref in enumerate((kv0_ref, kv1_ref, kv2_ref)):

        @pl.when(table_ref[b * 3 + slot] >= 0)
        def _():
            kv = kv_ref[0].reshape(BLOCK, 2 * HD)
            m, l, acc = attend(q, kv, None, m_ref[...], l_ref[...], acc_ref[...])
            m_ref[...] = m
            l_ref[...] = l
            acc_ref[...] = acc

    out = (acc_ref[...] / l_ref[...]).astype(jnp.bfloat16)
    for h in range(SHARE):
        o_ref[:, h * HD : (h + 1) * HD] = out[h * ROWS : (h + 1) * ROWS]


def local(queries, key_states, value_states, key_picks, positions):
    local_rows = queries.shape[0]
    kv_heads = key_states.shape[1] // HD
    query_heads = queries.shape[1] // HD
    head_devices = lax.axis_size("head")
    across = [[SHARE * g + r for g in range(kv_heads)] for r in range(SHARE)]
    within = [[SHARE * g + r for r in range(SHARE)] for g in range(kv_heads)]
    rank = lax.axis_index("head") % SHARE

    angles = positions.astype(jnp.float32)[:, None] * frequency_table(HD)[None, :]
    cosine = jnp.cos(angles)
    sine = jnp.sin(angles)
    cosine = jnp.concatenate([cosine, cosine], axis=1)
    sine = jnp.concatenate([-sine, sine], axis=1)

    sent_kv = pl.pallas_call(
        lambda *refs: kv_kernel(kv_heads, *refs),
        out_shape=jax.ShapeDtypeStruct((kv_heads, local_rows, 2 * HD), jnp.bfloat16),
        name="rope_kv",
    )(cosine, sine, key_states, value_states)
    part_kv = lax.all_to_all(
        sent_kv, "head", split_axis=0, concat_axis=0, axis_index_groups=across, tiled=True
    )
    blocks = part_kv.shape[0]
    own_kv = lax.all_gather(part_kv, "head", axis=0, axis_index_groups=within)

    first_block = lax.axis_index("seq") * blocks
    all_blocks = key_picks.shape[0]
    picks = key_picks.shape[1]
    public = min(picks, blocks)
    block_ids = jnp.arange(all_blocks, dtype=jnp.int32)
    block_group = block_ids // blocks
    picked_later = (key_picks[:, :, None] == block_ids[None, None, :]) & (
        block_group[:, None, None] > block_group[None, None, :]
    )
    is_public = jnp.any(picked_later, axis=(0, 1))
    slot_rank = (
        jnp.cumsum(is_public.reshape(-1, blocks).astype(jnp.int32), axis=1) - 1
    ).reshape(-1)
    place = block_group * public + slot_rank
    own_public = lax.dynamic_slice_in_dim(is_public, first_block, blocks, 0)
    own_rank = lax.dynamic_slice_in_dim(slot_rank, first_block, blocks, 0)
    slot_ids = jnp.arange(public, dtype=jnp.int32)
    chosen = jnp.sum(
        jnp.where(
            own_public[None, :] & (own_rank[None, :] == slot_ids[:, None]),
            jnp.arange(blocks, dtype=jnp.int32)[None, :],
            0,
        ),
        axis=1,
    )
    outgoing = jnp.concatenate(
        [lax.dynamic_slice_in_dim(own_kv, chosen[p], 1, 1) for p in range(public)], axis=1
    )
    outgoing = jnp.transpose(outgoing, (1, 0, 2, 3))
    held_kv = lax.all_gather(outgoing, "seq", axis=0, tiled=True)

    own_picks = lax.dynamic_slice_in_dim(key_picks, first_block, blocks, 0)
    row_block = first_block + jnp.arange(blocks, dtype=jnp.int32)[:, None]
    near = (own_picks >= first_block) & (own_picks < row_block)
    near_table = jnp.where(near, own_picks - first_block, -1).reshape(-1)
    far = own_picks < first_block
    pick_place = jnp.sum(
        jnp.where(own_picks[:, :, None] == block_ids[None, None, :], place[None, None, :], 0),
        axis=2,
    )
    far_table = jnp.where(far, pick_place, -1).reshape(-1)

    turned_queries = pl.pallas_call(
        lambda *refs: rope_kernel(query_heads, *refs),
        out_shape=jax.ShapeDtypeStruct(queries.shape, jnp.bfloat16),
        name="rope_q",
    )(cosine, sine, queries)
    group_queries = lax.all_to_all(
        turned_queries, "head", split_axis=1, concat_axis=0, axis_index_groups=across, tiled=True
    )
    tall = SHARE * ROWS
    wide = SHARE * HD
    stat = jax.ShapeDtypeStruct((blocks, tall, 1), jnp.float32)
    acc, m, l = pl.pallas_call(
        near_kernel,
        out_shape=(jax.ShapeDtypeStruct((blocks, tall, HD), jnp.float32), stat, stat),
        grid_spec=pltpu.PrefetchScalarGridSpec(
            num_scalar_prefetch=2,
            grid=(blocks,),
            in_specs=[
                pl.BlockSpec((ROWS, wide), lambda b, t, r: (b, 0)),
                pl.BlockSpec(own_kv.shape, lambda b, t, r: (0, 0, 0, 0)),
            ],
            out_specs=(
                pl.BlockSpec((1, tall, HD), lambda b, t, r: (b, 0, 0)),
                pl.BlockSpec((1, tall, 1), lambda b, t, r: (b, 0, 0)),
                pl.BlockSpec((1, tall, 1), lambda b, t, r: (b, 0, 0)),
            ),
        ),
        name="near_attention",
    )(near_table, rank.reshape(1), group_queries, own_kv)

    def held_spec(slot):
        return pl.BlockSpec(
            (1, SHARE, ROWS, 2 * HD), lambda b, t: (jnp.maximum(t[b * 3 + slot], 0), 0, 0, 0)
        )

    attended = pl.pallas_call(
        far_kernel,
        out_shape=jax.ShapeDtypeStruct(group_queries.shape, jnp.bfloat16),
        grid_spec=pltpu.PrefetchScalarGridSpec(
            num_scalar_prefetch=1,
            grid=(blocks,),
            in_specs=[
                pl.BlockSpec((ROWS, wide), lambda b, t: (b, 0)),
                held_spec(0),
                held_spec(1),
                held_spec(2),
                pl.BlockSpec((1, tall, HD), lambda b, t: (b, 0, 0)),
                pl.BlockSpec((1, tall, 1), lambda b, t: (b, 0, 0)),
                pl.BlockSpec((1, tall, 1), lambda b, t: (b, 0, 0)),
            ],
            out_specs=pl.BlockSpec((ROWS, wide), lambda b, t: (b, 0)),
            scratch_shapes=[
                pltpu.VMEM((tall, HD), jnp.float32),
                pltpu.VMEM((tall, 1), jnp.float32),
                pltpu.VMEM((tall, 1), jnp.float32),
            ],
        ),
        name="far_attention",
    )(far_table, group_queries, held_kv, held_kv, held_kv, acc, m, l)
    return lax.all_to_all(
        attended, "head", split_axis=0, concat_axis=1, axis_index_groups=across, tiled=True
    )


def solution(mesh):
    in_specs = (
        P(("seq", "head"), None),
        P(("seq", "head"), None),
        P(("seq", "head"), None),
        P(),
        P(("seq", "head")),
    )
    out_specs = P(("seq", "head"), None)
    return jax.shard_map(local, mesh=mesh, in_specs=in_specs, out_specs=out_specs, check_vma=False)
```

time: 671 us -> 313 us (0.47)
  the two profiles are of different devices: /device:TPU:54 before, /device:TPU:10 now
where the time goes in v1:
time: 313 us; the launch traced here: 312 us
  blocking collectives  110 us (35%)
  waiting for transfers between devices  96.5 us (31%)
  Pallas kernels  62.3 us (20%)
  between operations  19.5 us (6%)
  starting transfers between devices  12 us (4%)
  local copies, waits for them, and re-layouts  8.91 us (3%)
    all_to_all x1, blocking collectives, local(): lax.all_to_all(attended, 'head', split_axis=0, concat_axis=1, axis_index_...  65.1 us
    all_to_all x1, waiting for transfers between devices, local(): lax.all_to_all(turned_queries, 'head', split_axis=1, concat_axis=0, axis_...  53.8 us
    pallas_call x1, Pallas kernels, local(): pl.pallas_call(far_kernel, out_shape=jax.ShapeDtypeStruct(group_queries.s...  46.5 us
    all_to_all x1, blocking collectives, local(): lax.all_to_all(sent_kv, 'head', split_axis=0, concat_axis=0, axis_index_g...  44.9 us
    all_gather x1, waiting for transfers between devices, local(): own_kv = lax.all_gather(part_kv, 'head', axis=0, axis_index_groups=within)  42.7 us
    all_to_all x1, starting transfers between devices, local(): lax.all_to_all(turned_queries, 'head', split_axis=1, concat_axis=0, axis_...  12 us
    pallas_call x1, Pallas kernels, local(): pl.pallas_call(near_kernel, out_shape=(jax.ShapeDtypeStruct((blocks, tall...  10.9 us
  transfers between devices with their start and end apart: 3, of which 2 were waited for; matrix products, arithmetic and copies ran while one was open for 2% of the time, Pallas kernels for 4%

profile of v1, /device:TPU:10, one launch (start us, length us, event | category | flops | bytes accessed | tf_op | source)
XLA Modules:
  0.0 311.8 jit_solution(16149114374368336753)
XLA Ops:
  6.6 0.7 convert_element_type.11
  7.2 0.3 fusion.2
  7.5 0.8 pad_maximum_fusion
  8.3 2.1 rope_kv.1
  10.4 44.9 %all_to_all.43 = bf16[8,128,256]{2,1,0:T(8,128)(2,1)} all-to-all(bf16[8,128,256]{2,1,0:T(8,128)(2,1)} %rope_kv.1), channel_id=1, replica_groups={{0,4,8,12,16,20,24,28},{1,5,9,13,17,21,25,29},{2,6,10,14,18,22,26,30},{..., dimensions={0} | all-to-all | bytes 1048576 | tf_op jit(solution)/shard_map/all_to_all | solution.py:135
  55.5 0.1 fusion.1
  55.7 0.2 reduce_window_sum.11
  56.1 0.1 select_reduce_fusion.1
  56.3 0.7 fusion.4
  62.9 42.7 %all-gather.6.cloned.1.call-done = bf16[32,128,256]{2,1,0:T(8,128)(2,1)} async-done(((bf16[8,128,256]{2,1,0:T(8,128)(2,1)}), bf16[32,128,256]{2,1,0:T(8,128)(2,1)}) %all-gather.6.cloned.1.call-update) | async-done | bytes 2097168 | tf_op jit(solution)/shard_map/all_gather | solution.py:139
  105.6 1.2 constant_dynamic-slice_fusion.2
  106.9 0.9 copy.31
  107.8 2.8 rope_q.1
  110.6 2.3 copy.37
  112.9 12.0 %all-to-all-start = ((bf16[128,8,512]{2,0,1:T(8,128)(2,1)}), bf16[128,8,512]{2,0,1:T(8,128)(2,1)S(1)}, u32[]{:S(2)}, u32[]{:S(2)}) async-start(bf16[128,8,512]{2,0,1:T(8,128)(2,1)} %bitcast.17), calls=%async_computation | async-start | bytes 2097152 | tf_op jit(solution)/shard_map/all_to_all | solution.py:188
  125.1 0.6 reshape.120.table_ref
  125.7 0.2 select_reduce_fusion
  126.0 0.7 reshape.119.table_ref
  126.6 53.8 %all-to-all-done = bf16[128,8,512]{2,0,1:T(8,128)(2,1)S(1)} async-done(((bf16[128,8,512]{2,0,1:T(8,128)(2,1)}), bf16[128,8,512]{2,0,1:T(8,128)(2,1)S(1)}, u32[]{:S(2)}, u32[]{:S(2)}) %all-to-all-start) | async-done | bytes 1048608 | tf_op jit(solution)/shard_map/all_to_all | solution.py:188
  180.5 1.0 copy-done
  181.4 10.9 %near_attention.1 = (f32[8,512,128]{2,1,0:T(8,128)}, f32[8,512,1]{2,1,0:T(8,128)}, f32[8,512,1]{2,1,0:T(8,128)}) custom-call(s32[24]{0:T(128)} %reshape.120.table_ref, s32[1]{0:T(128)} %bitcast.7.rank_ref, bf16[1024,512]{1,0:T(8,128)(2,1)} %bitcast.18, bf16[4,8,128,256]{3,2,1,0:T(8,128)(2,1)} %bitcast.24), custom_call_target="tpu_custom_call" | custom-call | tf_op jit(solution)/shard_map/near_attention/pallas_call | solution.py:194
  192.4 46.5 %far_attention.1 = bf16[1024,512]{1,0:T(8,128)(2,1)} custom-call(s32[24]{0:T(128)} %reshape.119.table_ref, bf16[1024,512]{1,0:T(8,128)(2,1)} %bitcast.19, bf16[48,4,128,256]{3,2,1,0:T(8,128)(2,1)} %all-gather.4.cloned.1.call-done.kv0_ref.kv1_ref.kv2_ref, bf16[48,4,128,256]{3,2,1,0:T(8,128)(2,1)} %all-gather.4.cloned.1.call-done.kv0_ref.kv1_ref.kv2_ref, ...), custom_call_target="tpu_custom_call" | custom-call | tf_op jit(solution)/shard_map/far_attention/pallas_call | solution.py:218
  238.8 65.1 %all_to_all.44 = bf16[8,128,512]{2,1,0:T(8,128)(2,1)S(1)} all-to-all(bf16[8,128,512]{2,1,0:T(8,128)(2,1)} %bitcast.20), channel_id=1, replica_groups={{0,4,8,12,16,20,24,28},{1,5,9,13,17,21,25,29},{2,6,10,14,18,22,26,30},{..., dimensions={0} | all-to-all | bytes 2097152 | tf_op jit(solution)/shard_map/all_to_all | solution.py:242
  303.9 1.1 copy.35
  (24 shorter events, 0.9 us)
Async XLA Ops:
  6.5 49.0 %copy-start.1 = (s32[128,3]{0,1:T(4,128)S(1)}, s32[128,3]{0,1:T(4,128)}, u32[]{:S(2)}) copy-start(s32[128,3]{0,1:T(4,128)} %param.8) | copy-start | bytes 4612
  6.5 99.1 %all-gather.6.cloned.1.call-start = ((), (), s32[]{:S(2)}) async-start(), calls=%async_computation.4 | async-start | bytes 2621440 | tf_op jit(solution)/shard_map/all_gather | solution.py:139
  55.3 137.0 %all-gather.4.cloned.1.call-start = ((), (), s32[]{:S(2)}) async-start(), calls=%async_computation.3 | async-start | bytes 13369344 | tf_op jit(solution)/shard_map/all_gather | solution.py:170
  112.9 67.6 %all-to-all-start = ((bf16[128,8,512]{2,0,1:T(8,128)(2,1)}), bf16[128,8,512]{2,0,1:T(8,128)(2,1)S(1)}, u32[]{:S(2)}, u32[]{:S(2)}) async-start(bf16[128,8,512]{2,0,1:T(8,128)(2,1)} %bitcast.17), calls=%async_computation | async-start | bytes 2097152 | tf_op jit(solution)/shard_map/all_to_all | solution.py:188
  180.5 1.0 copy-start
Sparse Core Ops, SparseCore 0:
  55.4 50.0 all-gather.5
  107.9 82.1 all-gather.3

commit v2 on v1

v2 whole, which is shorter than its diff:
```python
import functools
import math

import jax
import jax.numpy as jnp
from jax import lax
from jax.experimental import pallas as pl
from jax.experimental.pallas import tpu as pltpu
from jax.sharding import PartitionSpec as P

HD = 128
BLOCK = 512
SHARE = 4
ROWS = BLOCK // SHARE
LOWEST = -1e30
SCALE = 1.0 / math.sqrt(HD)
MESH = pl.DeviceIdType.MESH
LOG2E = math.log2(math.e)


def frequency_table(columns):
    inverse = 1.0 / 500000.0 ** (jnp.arange(0, columns, 2, dtype=jnp.float32) / columns)
    wavelength = 2.0 * math.pi / inverse
    smooth = (8192.0 / wavelength - 1.0) / 3.0
    blended = (1.0 - smooth) * inverse / 8.0 + smooth * inverse
    return jnp.where(
        wavelength < 2048.0, inverse, jnp.where(wavelength > 8192.0, inverse / 8.0, blended)
    )


def rope_kernel(heads, cos_ref, sin_ref, x_ref, o_ref):
    cosine = cos_ref[...]
    sine = sin_ref[...]
    for h in range(heads):
        x = x_ref[:, h * HD : (h + 1) * HD].astype(jnp.float32)
        turned = x * cosine + pltpu.roll(x, HD // 2, 1) * sine
        o_ref[:, h * HD : (h + 1) * HD] = turned.astype(jnp.bfloat16)


def kv_kernel(heads, cos_ref, sin_ref, k_ref, v_ref, o_ref):
    cosine = cos_ref[...]
    sine = sin_ref[...]
    for h in range(heads):
        x = k_ref[:, h * HD : (h + 1) * HD].astype(jnp.float32)
        turned = x * cosine + pltpu.roll(x, HD // 2, 1) * sine
        o_ref[h, :, :HD] = turned.astype(jnp.bfloat16)
        o_ref[h, :, HD:] = v_ref[:, h * HD : (h + 1) * HD]


def attend(q, kv, mask, bias, carry):
    s = lax.dot_general(
        q, kv[:, :HD], (((1,), (1,)), ((), ())), preferred_element_type=jnp.float32
    ) * (SCALE * LOG2E)
    if mask is not None:
        s = jnp.where(mask, s, LOWEST)
    if bias is not None:
        s = s + bias
    top = jnp.max(s, axis=1, keepdims=True)
    if carry is not None:
        top = jnp.maximum(carry[0], top)
    p = jnp.exp2(s - top)
    total = jnp.sum(p, axis=1, keepdims=True)
    product = jnp.dot(p.astype(jnp.bfloat16), kv[:, HD:], preferred_element_type=jnp.float32)
    if carry is not None:
        keep = jnp.exp2(carry[0] - top)
        total = total + carry[1] * keep
        product = product + carry[2] * keep
    return top, total, product


def group_kernel(
    blocks,
    public,
    ring,
    chosen_ref,
    place_ref,
    bias_ref,
    kv_in,
    q_in,
    o_ref,
    own_kv,
    kv_all,
    q_all,
    out_buf,
    send_sem,
    kv_sem,
    fy_sem,
    fz_sem,
    q_sem,
    ag_sem,
    o_sem,
    local_sem,
):
    s = lax.axis_index("seq")
    d = lax.axis_index("head")
    g, r = d // SHARE, d % SHARE
    x, y_lo, core = s // 4, (s // 2) % 2, s % 2
    z_par, y_hi = r // 2, r % 2
    wide = SHARE * HD
    heads = blocks

    def at_x(step):
        return ((x + step + ring) % ring) * 4 + s % 4

    def across(step):
        return (s, ((g + step + heads) % heads) * SHARE + r)

    y_flip = d + 1 - 2 * y_hi
    y_peer = (s, y_flip)
    z_peer = (s, d + 2 - 4 * z_par)
    s_flip = s + 2 - 4 * y_lo
    y_near, y_far = (s_flip, d), (s_flip, y_flip)
    core_peer = (s + 1 - 2 * core, d)
    x_next, x_last = (at_x(1), d), (at_x(-1), d)
    partners = [across(j) for j in range(1, heads)]
    partners += [y_peer, z_peer, y_near, y_far, core_peer, x_next, x_last]

    barrier = pltpu.get_barrier_semaphore()
    for peer in partners:
        pl.semaphore_signal(barrier, inc=1, device_id=peer, device_id_type=MESH)
    pl.semaphore_wait(barrier, len(partners))

    pending = []

    def send(source, target, arrival, peer):
        copy = pltpu.make_async_remote_copy(
            src_ref=source,
            dst_ref=target,
            send_sem=send_sem.at[len(pending)],
            recv_sem=arrival,
            device_id=peer,
            device_id_type=MESH,
        )
        copy.start()
        pending.append(copy)

    def arrived(region, arrival):
        pltpu.make_async_remote_copy(
            src_ref=region,
            dst_ref=region,
            send_sem=send_sem.at[0],
            recv_sem=arrival,
            device_id=core_peer,
            device_id_type=MESH,
        ).wait_recv()

    def away(step):
        return (g + step + heads) % heads

    order = []
    for j in range(1, heads // 2 + 1):
        order += [j] if 2 * j == heads else [j, heads - j]

    own_local = pltpu.make_async_copy(kv_in.at[g], own_kv.at[g, r], local_sem.at[0])
    own_local.start()
    for j in order:
        send(kv_in.at[away(j)], own_kv.at[g, r], kv_sem.at[j], across(j))
    query_local = pltpu.make_async_copy(
        q_in.at[:, pl.ds(pl.multiple_of(g * wide, wide), wide)], q_all.at[g], local_sem.at[1]
    )
    query_local.start()
    r_y, r_z = r + 1 - 2 * y_hi, r + 2 - 4 * z_par
    r_zy = r_y + 2 - 4 * z_par
    for j in [0] + order:
        region = own_kv.at[away(-j), r]
        if j == 0:
            own_local.wait()
        else:
            arrived(region, kv_sem.at[j])
        send(region, region, fy_sem.at[j], y_peer)
        send(region, region, fz_sem.at[0, j], z_peer)
    for j in [0] + order:
        region = own_kv.at[away(-j), r_y]
        arrived(region, fy_sem.at[j])
        send(region, region, fz_sem.at[1, j], z_peer)
    for j in order:
        send(
            q_in.at[:, pl.ds(pl.multiple_of(away(j) * wide, wide), wide)],
            q_all.at[g],
            q_sem.at[j],
            across(j),
        )
    for j in [0] + order:
        arrived(own_kv.at[away(-j), r_z], fz_sem.at[0, j])
        arrived(own_kv.at[away(-j), r_zy], fz_sem.at[1, j])

    for p in range(public):
        kv_all[blocks + public * s + p] = own_kv[chosen_ref[p]]
    own_copy = pltpu.make_async_copy(own_kv, kv_all.at[pl.ds(0, blocks)], local_sem.at[2])
    own_copy.start()

    def unit(where, half=None):
        rows = pl.ds(blocks + public * where, public)
        if half is None:
            return kv_all.at[rows]
        return kv_all.at[rows, pl.ds(half * (SHARE // 2), SHARE // 2)]

    steps = (0, -1, 1, 2)
    whole = unit(s)
    send(whole, whole, ag_sem.at[0], x_next)
    send(whole, whole, ag_sem.at[1], x_last)
    for half, peer in ((0, y_near), (1, y_far)):
        region = unit(s, half)
        send(region, region, ag_sem.at[4 + half], peer)
    send(whole, whole, ag_sem.at[12], core_peer)
    for k, half, peer in ((1, 0, x_next), (2, 1, x_last)):
        where = at_x(steps[k])
        arrived(unit(where), ag_sem.at[k - 1])
        region = unit(where, half)
        send(region, region, ag_sem.at[2 + half], peer)
        for part, side in ((0, y_near), (1, y_far)):
            region = unit(where, part)
            send(region, region, ag_sem.at[4 + 2 * k + part], side)
        send(unit(where), unit(where), ag_sem.at[12 + k], core_peer)
    for half, peer in ((0, y_near), (1, y_far)):
        region = unit(at_x(2), half)
        arrived(region, ag_sem.at[2 + half])
        send(region, region, ag_sem.at[10 + half], peer)
        send(region, region, ag_sem.at[15 + half], core_peer)
    for k in range(4):
        where = at_x(steps[k]) + 2 - 4 * y_lo
        for half in range(2):
            region = unit(where, half)
            arrived(region, ag_sem.at[4 + 2 * k + half])
            send(region, region, ag_sem.at[17 + 2 * k + half], core_peer)
    other = 1 - 2 * core
    for k in range(3):
        arrived(unit(at_x(steps[k]) + other), ag_sem.at[12 + k])
    for half in range(2):
        arrived(unit(at_x(2) + other, half), ag_sem.at[15 + half])
    for k in range(4):
        where = at_x(steps[k]) + 2 - 4 * y_lo + other
        for half in range(2):
            arrived(unit(where, half), ag_sem.at[17 + 2 * k + half])
    own_copy.wait()
    query_local.wait()
    for j in order:
        arrived(q_all.at[away(-j)], q_sem.at[j])

    tall = SHARE * ROWS
    row = lax.broadcasted_iota(jnp.int32, (tall, BLOCK), 0) % ROWS + r * ROWS
    col = lax.broadcasted_iota(jnp.int32, (tall, BLOCK), 1)
    causal = row >= col
    mine = pl.ds(pl.multiple_of(g * wide, wide), wide)
    base = len(pending)

    def home(j):
        return pltpu.make_async_remote_copy(
            src_ref=out_buf.at[j],
            dst_ref=o_ref.at[:, mine],
            send_sem=send_sem.at[base + j],
            recv_sem=o_sem.at[j],
            device_id=(s, ((g + 1 + j) % heads) * SHARE + r),
            device_id_type=MESH,
        )

    def one_block(j, _):
        b = (g + 1 + j) % heads
        q = jnp.concatenate([q_all[b, :, h * HD : (h + 1) * HD] for h in range(SHARE)], axis=0)
        carry = attend(q, kv_all[b].reshape(BLOCK, 2 * HD), causal, None, None)

        @pl.when(j > 0)
        def _():
            home(j - 1).start()

        for slot in range(3):
            kv = kv_all[place_ref[b * 3 + slot]].reshape(BLOCK, 2 * HD)
            carry = attend(q, kv, None, bias_ref[b * 3 + slot], carry)
        out = (carry[2] / carry[1]).astype(jnp.bfloat16)
        for h in range(SHARE):
            out_buf[j, :, h * HD : (h + 1) * HD] = out[h * ROWS : (h + 1) * ROWS]
        return 0

    lax.fori_loop(0, heads, one_block, 0)
    last = pltpu.make_async_copy(out_buf.at[heads - 1], o_ref.at[:, mine], local_sem.at[3])
    last.start()
    for copy in pending:
        copy.wait_send()
    for j in range(heads - 1):
        columns = pl.ds(pl.multiple_of(away(-1 - j) * wide, wide), wide)
        arrived(o_ref.at[:, columns], o_sem.at[j])
        home(j).wait_send()
    last.wait()


def local(queries, key_states, value_states, key_picks, positions):
    local_rows = queries.shape[0]
    kv_heads = key_states.shape[1] // HD
    query_heads = queries.shape[1] // HD

    angles = positions.astype(jnp.float32)[:, None] * frequency_table(HD)[None, :]
    cosine = jnp.cos(angles)
    sine = jnp.sin(angles)
    cosine = jnp.concatenate([cosine, cosine], axis=1)
    sine = jnp.concatenate([-sine, sine], axis=1)

    sent_kv = pl.pallas_call(
        lambda *refs: kv_kernel(kv_heads, *refs),
        out_shape=jax.ShapeDtypeStruct((kv_heads, local_rows, 2 * HD), jnp.bfloat16),
        name="rope_kv",
    )(cosine, sine, key_states, value_states)
    turned_queries = pl.pallas_call(
        lambda *refs: rope_kernel(query_heads, *refs),
        out_shape=jax.ShapeDtypeStruct(queries.shape, jnp.bfloat16),
        name="rope_q",
    )(cosine, sine, queries)

    groups = lax.axis_size("seq")
    all_blocks, picks = key_picks.shape
    blocks = all_blocks // groups
    first_block = lax.axis_index("seq") * blocks
    public = min(picks, blocks)
    block_ids = jnp.arange(all_blocks, dtype=jnp.int32)
    block_group = block_ids // blocks
    picked_later = (key_picks[:, :, None] == block_ids[None, None, :]) & (
        block_group[:, None, None] > block_group[None, None, :]
    )
    is_public = jnp.any(picked_later, axis=(0, 1))
    slot_rank = (
        jnp.cumsum(is_public.reshape(-1, blocks).astype(jnp.int32), axis=1) - 1
    ).reshape(-1)
    place = block_group * public + slot_rank
    own_public = lax.dynamic_slice_in_dim(is_public, first_block, blocks, 0)
    own_rank = lax.dynamic_slice_in_dim(slot_rank, first_block, blocks, 0)
    slot_ids = jnp.arange(public, dtype=jnp.int32)
    chosen = jnp.sum(
        jnp.where(
            own_public[None, :] & (own_rank[None, :] == slot_ids[:, None]),
            jnp.arange(blocks, dtype=jnp.int32)[None, :],
            0,
        ),
        axis=1,
    )
    own_picks = lax.dynamic_slice_in_dim(key_picks, first_block, blocks, 0)
    row_block = first_block + jnp.arange(blocks, dtype=jnp.int32)[:, None]
    near = (own_picks >= first_block) & (own_picks < row_block)
    far = own_picks < first_block
    pick_place = jnp.sum(
        jnp.where(own_picks[:, :, None] == block_ids[None, None, :], place[None, None, :], 0),
        axis=2,
    )
    held = jnp.where(near, own_picks - first_block, jnp.where(far, blocks + pick_place, 0))
    bias = jnp.where(near | far, 0.0, LOWEST).astype(jnp.float32)

    smem = pl.BlockSpec(memory_space=pltpu.SMEM)
    anywhere = pl.BlockSpec(memory_space=pl.ANY)
    copies = 2 * (kv_heads - 1) + 3 * kv_heads + 25 + (kv_heads - 1)
    return pl.pallas_call(
        functools.partial(group_kernel, blocks, public, groups // 4),
        out_shape=jax.ShapeDtypeStruct(queries.shape, jnp.bfloat16),
        in_specs=[smem, smem, smem, anywhere, anywhere],
        out_specs=anywhere,
        scratch_shapes=[
            pltpu.VMEM((blocks, SHARE, ROWS, 2 * HD), jnp.bfloat16),
            pltpu.VMEM((blocks + groups * public, SHARE, ROWS, 2 * HD), jnp.bfloat16),
            pltpu.VMEM((blocks, ROWS, SHARE * HD), jnp.bfloat16),
            pltpu.VMEM((blocks, ROWS, SHARE * HD), jnp.bfloat16),
            pltpu.SemaphoreType.DMA((copies,)),
            pltpu.SemaphoreType.DMA((kv_heads,)),
            pltpu.SemaphoreType.DMA((kv_heads,)),
            pltpu.SemaphoreType.DMA((2, kv_heads)),
            pltpu.SemaphoreType.DMA((kv_heads,)),
            pltpu.SemaphoreType.DMA((25,)),
            pltpu.SemaphoreType.DMA((kv_heads,)),
            pltpu.SemaphoreType.DMA((4,)),
        ],
        compiler_params=pltpu.CompilerParams(
            collective_id=0, has_side_effects=True, vmem_limit_bytes=48 << 20
        ),
        name="group_attention",
    )(chosen, held.reshape(-1), bias.reshape(-1), sent_kv, turned_queries)


def solution(mesh):
    in_specs = (
        P(("seq", "head"), None),
        P(("seq", "head"), None),
        P(("seq", "head"), None),
        P(),
        P(("seq", "head")),
    )
    out_specs = P(("seq", "head"), None)
    return jax.shard_map(local, mesh=mesh, in_specs=in_specs, out_specs=out_specs, check_vma=False)
```

time: 313 us -> 198 us (0.63)
  the two profiles are of different devices: /device:TPU:10 before, /device:TPU:1 now
where the time goes in v2:
time: 198 us; the launch traced here: 197 us
  Pallas kernels  191 us (96%)
  local copies, waits for them, and re-layouts  4.18 us (2%)
    pallas_call x1, Pallas kernels, local(): pl.pallas_call(functools.partial(group_kernel, blocks, public, groups //...  186 us

profile of v2, /device:TPU:1, one launch (start us, length us, event | category | flops | bytes accessed | tf_op | source)
XLA Modules:
  0.0 197.4 jit_solution(10304680186080305398)
XLA Ops:
  0.0 0.6 copy-done.3
  0.7 0.7 copy-done.2
  1.3 0.1 or_select_fusion
  1.4 0.1 copy.15
  1.5 0.1 reshape.111.bias_ref
  1.6 0.1 broadcast_compare_fusion
  1.7 0.1 fusion.1
  1.8 0.1 dynamic_slice.9
  1.9 0.1 reshape.112
  2.0 0.2 reduce_window_sum.11
  2.1 0.1 sub.30
  2.2 0.1 dynamic_slice.10
  2.3 0.1 select_reduce_fusion.1.chosen_ref
  2.5 0.2 select_reduce_fusion
  2.7 0.1 copy.14
  2.8 0.1 reshape.110.place_ref
  2.9 0.3 fusion.2
  3.2 0.8 pad_maximum_fusion
  3.9 2.1 %rope_kv.1.kv_in = bf16[8,128,256]{2,1,0:T(8,128)(2,1)} custom-call(f32[128,128]{1,0:T(8,128)} %get-tuple-element.10.refs_0_, f32[128,128]{1,0:T(8,128)} %get-tuple-element.11.refs_1_, bf16[128,1024]{1,0:T(8,128)(2,1)} %refs_2_.2, bf16[128,1024]{1,0:T(8,128)(2,1)} %refs_3_.1), custom_call_target="tpu_custom_call" | custom-call | tf_op jit(solution)/shard_map/rope_kv/pallas_call | solution.py:297
  6.0 2.8 %rope_q.1.q_in = bf16[128,4096]{1,0:T(8,128)(2,1)} custom-call(f32[128,128]{1,0:T(8,128)} %get-tuple-element.10.refs_0_, f32[128,128]{1,0:T(8,128)} %get-tuple-element.11.refs_1_, bf16[128,4096]{1,0:T(8,128)(2,1)} %refs_2_.3), custom_call_target="tpu_custom_call" | custom-call | tf_op jit(solution)/shard_map/rope_q/pallas_call | solution.py:302
  8.9 0.0 copy-done.1
  8.9 1.2 copy-done
  10.1 186.4 %group_attention.1 = bf16[128,4096]{1,0:T(8,128)(2,1)S(1)} custom-call(s32[3]{0:T(128)S(1)} %select_reduce_fusion.1.chosen_ref, s32[24]{0:T(128)S(1)} %reshape.110.place_ref, f32[24]{0:T(128)S(1)} %reshape.111.bias_ref, bf16[8,128,256]{2,1,0:T(8,128)(2,1)S(1)} %copy-done.1, bf16[128,4096]{1,0:T(8,128)(2,1)S(1)} %copy-done), custom_call_target="tpu_custom_call" | custom-call | tf_op jit(solution)/shard_map/group_attention/pallas_call | solution.py:348
  196.5 1.0 copy.17
  (12 shorter events, 0.1 us)
Async XLA Ops:
  0.0 0.7 copy-start.3
  0.7 0.7 copy-start.2
  6.0 2.8 %copy-start.1 = (bf16[8,128,256]{2,1,0:T(8,128)(2,1)S(1)}, bf16[8,128,256]{2,1,0:T(8,128)(2,1)}, u32[]{:S(2)}) copy-start(bf16[8,128,256]{2,1,0:T(8,128)(2,1)} %rope_kv.1.kv_in) | copy-start | bytes 1572868
  8.9 1.2 copy-start

commit v3 on v2

--- a/solution.py
+++ b/solution.py
@@ -78,7 +78,8 @@
     kv_in,
     q_in,
     o_ref,
-    own_kv,
+    own_a,
+    own_b,
     kv_all,
     q_all,
     out_buf,
@@ -151,28 +152,26 @@
     for j in range(1, heads // 2 + 1):
         order += [j] if 2 * j == heads else [j, heads - j]
 
-    own_local = pltpu.make_async_copy(kv_in.at[g], own_kv.at[g, r], local_sem.at[0])
+    own_local = pltpu.make_async_copy(kv_in.at[g], own_a.at[g, y_hi], local_sem.at[0])
     own_local.start()
     for j in order:
-        send(kv_in.at[away(j)], own_kv.at[g, r], kv_sem.at[j], across(j))
+        send(kv_in.at[away(j)], own_a.at[g, y_hi], kv_sem.at[j], across(j))
     query_local = pltpu.make_async_copy(
         q_in.at[:, pl.ds(pl.multiple_of(g * wide, wide), wide)], q_all.at[g], local_sem.at[1]
     )
     query_local.start()
-    r_y, r_z = r + 1 - 2 * y_hi, r + 2 - 4 * z_par
-    r_zy = r_y + 2 - 4 * z_par
     for j in [0] + order:
-        region = own_kv.at[away(-j), r]
+        region = own_a.at[away(-j), y_hi]
         if j == 0:
             own_local.wait()
         else:
             arrived(region, kv_sem.at[j])
-        send(region, region, fy_sem.at[j], y_peer)
-        send(region, region, fz_sem.at[0, j], z_peer)
+        send(region, own_b.at[away(-j), y_hi], fz_sem.at[j], z_peer)
+        send(region, region, fy_sem.at[0, j], y_peer)
     for j in [0] + order:
-        region = own_kv.at[away(-j), r_y]
-        arrived(region, fy_sem.at[j])
-        send(region, region, fz_sem.at[1, j], z_peer)
+        region = own_b.at[away(-j), y_hi]
+        arrived(region, fz_sem.at[j])
+        send(region, region, fy_sem.at[1, j], y_peer)
     for j in order:
         send(
             q_in.at[:, pl.ds(pl.multiple_of(away(j) * wide, wide), wide)],
@@ -180,59 +179,66 @@
             q_sem.at[j],
             across(j),
         )
-    for j in [0] + order:
-        arrived(own_kv.at[away(-j), r_z], fz_sem.at[0, j])
-        arrived(own_kv.at[away(-j), r_zy], fz_sem.at[1, j])
-
-    for p in range(public):
-        kv_all[blocks + public * s + p] = own_kv[chosen_ref[p]]
-    own_copy = pltpu.make_async_copy(own_kv, kv_all.at[pl.ds(0, blocks)], local_sem.at[2])
-    own_copy.start()
-
-    def unit(where, half=None):
+
+    half_rows = SHARE // 2
+    halves = (z_par, 1 - z_par)
+    steps = (0, -1, 1, 2)
+
+    def unit(where, h):
         rows = pl.ds(blocks + public * where, public)
-        if half is None:
-            return kv_all.at[rows]
-        return kv_all.at[rows, pl.ds(half * (SHARE // 2), SHARE // 2)]
-
-    steps = (0, -1, 1, 2)
-    whole = unit(s)
-    send(whole, whole, ag_sem.at[0], x_next)
-    send(whole, whole, ag_sem.at[1], x_last)
-    for half, peer in ((0, y_near), (1, y_far)):
-        region = unit(s, half)
-        send(region, region, ag_sem.at[4 + half], peer)
-    send(whole, whole, ag_sem.at[12], core_peer)
-    for k, half, peer in ((1, 0, x_next), (2, 1, x_last)):
-        where = at_x(steps[k])
-        arrived(unit(where), ag_sem.at[k - 1])
-        region = unit(where, half)
-        send(region, region, ag_sem.at[2 + half], peer)
-        for part, side in ((0, y_near), (1, y_far)):
-            region = unit(where, part)
-            send(region, region, ag_sem.at[4 + 2 * k + part], side)
-        send(unit(where), unit(where), ag_sem.at[12 + k], core_peer)
-    for half, peer in ((0, y_near), (1, y_far)):
-        region = unit(at_x(2), half)
-        arrived(region, ag_sem.at[2 + half])
-        send(region, region, ag_sem.at[10 + half], peer)
-        send(region, region, ag_sem.at[15 + half], core_peer)
+        return kv_all.at[rows, pl.ds(halves[h] * half_rows, half_rows)]
+
+    def x_arrival(k, h):
+        return ag_sem.at[2 * (k - 1) + h]
+
+    def y_arrival(k, h):
+        return ag_sem.at[6 + 2 * k + h]
+
+    def core_arrival(column, k, h):
+        return ag_sem.at[14 + 8 * column + 2 * k + h]
+
+    sides = (y_near, y_far)
+    own_copies = []
+    for h, own in ((0, own_a), (1, own_b)):
+        for j in [0] + order:
+            arrived(own.at[away(-j), 1 - y_hi], fy_sem.at[h, j])
+        part = pl.ds(halves[h] * half_rows, half_rows)
+        for p in range(public):
+            kv_all[blocks + public * s + p, part] = own[chosen_ref[p]]
+        own_copies.append(
+            pltpu.make_async_copy(own, kv_all.at[pl.ds(0, blocks), part], local_sem.at[2 + h])
+        )
+        own_copies[-1].start()
+        region = unit(s, h)
+        send(region, region, x_arrival(1, h), x_next)
+        send(region, region, x_arrival(2, h), x_last)
+        send(region, region, y_arrival(0, h), sides[h])
+        send(region, region, core_arrival(0, 0, h), core_peer)
+    for h in range(2):
+        for k, onward in ((1, x_next), (2, x_last)):
+            region = unit(at_x(steps[k]), h)
+            arrived(region, x_arrival(k, h))
+            if h == k - 1:
+                send(region, region, x_arrival(3, h), onward)
+            send(region, region, y_arrival(k, h), sides[h])
+            send(region, region, core_arrival(0, k, h), core_peer)
+    for h in range(2):
+        region = unit(at_x(2), h)
+        arrived(region, x_arrival(3, h))
+        send(region, region, y_arrival(3, h), sides[h])
+        send(region, region, core_arrival(0, 3, h), core_peer)
     for k in range(4):
-        where = at_x(steps[k]) + 2 - 4 * y_lo
-        for half in range(2):
-            region = unit(where, half)
-            arrived(region, ag_sem.at[4 + 2 * k + half])
-            send(region, region, ag_sem.at[17 + 2 * k + half], core_peer)
-    other = 1 - 2 * core
-    for k in range(3):
-        arrived(unit(at_x(steps[k]) + other), ag_sem.at[12 + k])
-    for half in range(2):
-        arrived(unit(at_x(2) + other, half), ag_sem.at[15 + half])
-    for k in range(4):
-        where = at_x(steps[k]) + 2 - 4 * y_lo + other
-        for half in range(2):
-            arrived(unit(where, half), ag_sem.at[17 + 2 * k + half])
-    own_copy.wait()
+        for h in range(2):
+            region = unit(at_x(steps[k]) + 2 - 4 * y_lo, h)
+            arrived(region, y_arrival(k, h))
+            send(region, region, core_arrival(1, k, h), core_peer)
+    for column in range(2):
+        for k in range(4):
+            where = at_x(steps[k]) + column * (2 - 4 * y_lo) + 1 - 2 * core
+            for h in range(2):
+                arrived(unit(where, h), core_arrival(column, k, h))
+    for copy in own_copies:
+        copy.wait()
     query_local.wait()
     for j in order:
         arrived(q_all.at[away(-j)], q_sem.at[j])
@@ -244,18 +250,21 @@
     mine = pl.ds(pl.multiple_of(g * wide, wide), wide)
     base = len(pending)
 
+    def offset(j):
+        return (1 - 2 * (j % 2)) * (heads // 2 - (j + 1) // 2)
+
     def home(j):
         return pltpu.make_async_remote_copy(
             src_ref=out_buf.at[j],
             dst_ref=o_ref.at[:, mine],
             send_sem=send_sem.at[base + j],
             recv_sem=o_sem.at[j],
-            device_id=(s, ((g + 1 + j) % heads) * SHARE + r),
+            device_id=across(offset(j)),
             device_id_type=MESH,
         )
 
     def one_block(j, _):
-        b = (g + 1 + j) % heads
+        b = away(offset(j))
         q = jnp.concatenate([q_all[b, :, h * HD : (h + 1) * HD] for h in range(SHARE)], axis=0)
         carry = attend(q, kv_all[b].reshape(BLOCK, 2 * HD), causal, None, None)
 
@@ -272,12 +281,12 @@
         return 0
 
     lax.fori_loop(0, heads, one_block, 0)
-    last = pltpu.make_async_copy(out_buf.at[heads - 1], o_ref.at[:, mine], local_sem.at[3])
+    last = pltpu.make_async_copy(out_buf.at[heads - 1], o_ref.at[:, mine], local_sem.at[4])
     last.start()
     for copy in pending:
         copy.wait_send()
     for j in range(heads - 1):
-        columns = pl.ds(pl.multiple_of(away(-1 - j) * wide, wide), wide)
+        columns = pl.ds(pl.multiple_of(away(-offset(j)) * wide, wide), wide)
         arrived(o_ref.at[:, columns], o_sem.at[j])
         home(j).wait_send()
     last.wait()
@@ -343,26 +352,28 @@
     bias = jnp.where(near | far, 0.0, LOWEST).astype(jnp.float32)
 
     smem = pl.BlockSpec(memory_space=pltpu.SMEM)
+    vmem = pl.BlockSpec(memory_space=pltpu.VMEM)
     anywhere = pl.BlockSpec(memory_space=pl.ANY)
-    copies = 2 * (kv_heads - 1) + 3 * kv_heads + 25 + (kv_heads - 1)
+    copies = 2 * (kv_heads - 1) + 3 * kv_heads + 30 + (kv_heads - 1)
     return pl.pallas_call(
         functools.partial(group_kernel, blocks, public, groups // 4),
         out_shape=jax.ShapeDtypeStruct(queries.shape, jnp.bfloat16),
-        in_specs=[smem, smem, smem, anywhere, anywhere],
+        in_specs=[smem, smem, smem, vmem, vmem],
         out_specs=anywhere,
         scratch_shapes=[
-            pltpu.VMEM((blocks, SHARE, ROWS, 2 * HD), jnp.bfloat16),
+            pltpu.VMEM((blocks, SHARE // 2, ROWS, 2 * HD), jnp.bfloat16),
+            pltpu.VMEM((blocks, SHARE // 2, ROWS, 2 * HD), jnp.bfloat16),
             pltpu.VMEM((blocks + groups * public, SHARE, ROWS, 2 * HD), jnp.bfloat16),
             pltpu.VMEM((blocks, ROWS, SHARE * HD), jnp.bfloat16),
             pltpu.VMEM((blocks, ROWS, SHARE * HD), jnp.bfloat16),
             pltpu.SemaphoreType.DMA((copies,)),
             pltpu.SemaphoreType.DMA((kv_heads,)),
-            pltpu.SemaphoreType.DMA((kv_heads,)),
             pltpu.SemaphoreType.DMA((2, kv_heads)),
             pltpu.SemaphoreType.DMA((kv_heads,)),
-            pltpu.SemaphoreType.DMA((25,)),
             pltpu.SemaphoreType.DMA((kv_heads,)),
-            pltpu.SemaphoreType.DMA((4,)),
+            pltpu.SemaphoreType.DMA((30,)),
+            pltpu.SemaphoreType.DMA((kv_heads,)),
+            pltpu.SemaphoreType.DMA((5,)),
         ],
         compiler_params=pltpu.CompilerParams(
             collective_id=0, has_side_effects=True, vmem_limit_bytes=48 << 20

time: 198 us -> 164 us (0.83)
  Pallas kernels: 191 us -> 157 us
    pallas_call x1, Pallas kernels: 186 us -> 152 us  [local(): pl.pallas_call(functools.partial(group_kernel, blocks, public, groups //...]
where the time goes in v3:
time: 164 us; the launch traced here: 163 us
  Pallas kernels  157 us (96%)
  local copies, waits for them, and re-layouts  4.18 us (3%)
  other arithmetic  1.92 us (1%)
    pallas_call x1, Pallas kernels, local(): pl.pallas_call(functools.partial(group_kernel, blocks, public, groups //...  152 us
    unnamed x9, local copies, waits for them, and re-layouts  3.51 us

profile of v3, /device:TPU:1, one launch (start us, length us, event | category | flops | bytes accessed | tf_op | source)
XLA Modules:
  0.0 163.4 jit_solution(16643333854705159950)
XLA Ops:
  0.0 0.6 copy-done.3
  0.7 0.7 copy-done.2
  1.3 0.1 or_select_fusion
  1.4 0.1 copy.15
  1.5 0.1 reshape.111.bias_ref
  1.6 0.1 broadcast_compare_fusion
  1.7 0.1 fusion.1
  1.8 0.1 dynamic_slice.9
  1.9 0.1 reshape.112
  2.0 0.2 reduce_window_sum.11
  2.1 0.1 sub.30
  2.2 0.1 dynamic_slice.10
  2.3 0.1 select_reduce_fusion.1.chosen_ref
  2.5 0.2 select_reduce_fusion
  2.7 0.1 copy.14
  2.8 0.1 reshape.110.place_ref
  2.9 0.3 fusion.2
  3.2 0.8 pad_maximum_fusion
  3.9 2.1 %rope_kv.1.kv_in = bf16[8,128,256]{2,1,0:T(8,128)(2,1)} custom-call(f32[128,128]{1,0:T(8,128)} %get-tuple-element.10.refs_0_, f32[128,128]{1,0:T(8,128)} %get-tuple-element.11.refs_1_, bf16[128,1024]{1,0:T(8,128)(2,1)} %refs_2_.2, bf16[128,1024]{1,0:T(8,128)(2,1)} %refs_3_.1), custom_call_target="tpu_custom_call" | custom-call | tf_op jit(solution)/shard_map/rope_kv/pallas_call | solution.py:306
  6.0 2.8 %rope_q.1.q_in = bf16[128,4096]{1,0:T(8,128)(2,1)} custom-call(f32[128,128]{1,0:T(8,128)} %get-tuple-element.10.refs_0_, f32[128,128]{1,0:T(8,128)} %get-tuple-element.11.refs_1_, bf16[128,4096]{1,0:T(8,128)(2,1)} %refs_2_.3), custom_call_target="tpu_custom_call" | custom-call | tf_op jit(solution)/shard_map/rope_q/pallas_call | solution.py:311
  8.9 0.0 copy-done.1
  8.9 1.2 copy-done
  10.1 152.4 %group_attention.1 = bf16[128,4096]{1,0:T(8,128)(2,1)S(1)} custom-call(s32[3]{0:T(128)S(1)} %select_reduce_fusion.1.chosen_ref, s32[24]{0:T(128)S(1)} %reshape.110.place_ref, f32[24]{0:T(128)S(1)} %reshape.111.bias_ref, bf16[8,128,256]{2,1,0:T(8,128)(2,1)S(1)} %copy-done.1, bf16[128,4096]{1,0:T(8,128)(2,1)S(1)} %copy-done), custom_call_target="tpu_custom_call" | custom-call | tf_op jit(solution)/shard_map/group_attention/pallas_call | solution.py:358
  162.5 1.0 copy.17
  (12 shorter events, 0.1 us)
Async XLA Ops:
  0.0 0.7 copy-start.3
  0.7 0.7 copy-start.2
  6.0 2.8 %copy-start.1 = (bf16[8,128,256]{2,1,0:T(8,128)(2,1)S(1)}, bf16[8,128,256]{2,1,0:T(8,128)(2,1)}, u32[]{:S(2)}) copy-start(bf16[8,128,256]{2,1,0:T(8,128)(2,1)} %rope_kv.1.kv_in) | copy-start | bytes 1572868
  8.9 1.2 copy-start

commit v4 on v3

--- a/solution.py
+++ b/solution.py
@@ -28,23 +28,9 @@
     )
 
 
-def rope_kernel(heads, cos_ref, sin_ref, x_ref, o_ref):
-    cosine = cos_ref[...]
-    sine = sin_ref[...]
-    for h in range(heads):
-        x = x_ref[:, h * HD : (h + 1) * HD].astype(jnp.float32)
-        turned = x * cosine + pltpu.roll(x, HD // 2, 1) * sine
-        o_ref[:, h * HD : (h + 1) * HD] = turned.astype(jnp.bfloat16)
-
-
-def kv_kernel(heads, cos_ref, sin_ref, k_ref, v_ref, o_ref):
-    cosine = cos_ref[...]
-    sine = sin_ref[...]
-    for h in range(heads):
-        x = k_ref[:, h * HD : (h + 1) * HD].astype(jnp.float32)
-        turned = x * cosine + pltpu.roll(x, HD // 2, 1) * sine
-        o_ref[h, :, :HD] = turned.astype(jnp.bfloat16)
-        o_ref[h, :, HD:] = v_ref[:, h * HD : (h + 1) * HD]
+def turn(x, cosine, sine):
+    x = x.astype(jnp.float32)
+    return (x * cosine + pltpu.roll(x, HD // 2, 1) * sine).astype(jnp.bfloat16)
 
 
 def attend(q, kv, mask, bias, carry):
@@ -75,9 +61,14 @@
     chosen_ref,
     place_ref,
     bias_ref,
+    cos_ref,
+    sin_ref,
+    k_ref,
+    v_ref,
+    q_ref,
+    o_ref,
     kv_in,
     q_in,
-    o_ref,
     own_a,
     own_b,
     kv_all,
@@ -119,6 +110,12 @@
     barrier = pltpu.get_barrier_semaphore()
     for peer in partners:
         pl.semaphore_signal(barrier, inc=1, device_id=peer, device_id_type=MESH)
+    raw = pltpu.make_async_copy(q_ref, q_in, local_sem.at[5])
+    raw.start()
+    for h in range(heads):
+        lanes = slice(h * HD, (h + 1) * HD)
+        kv_in[h, :, :HD] = turn(k_ref[:, lanes], cos_ref[...], sin_ref[...])
+        kv_in[h, :, HD:] = v_ref[:, lanes]
     pl.semaphore_wait(barrier, len(partners))
 
     pending = []
@@ -156,6 +153,10 @@
     own_local.start()
     for j in order:
         send(kv_in.at[away(j)], own_a.at[g, y_hi], kv_sem.at[j], across(j))
+    raw.wait()
+    for h in range(heads * SHARE):
+        lanes = slice(h * HD, (h + 1) * HD)
+        q_in[:, lanes] = turn(q_in[:, lanes], cos_ref[...], sin_ref[...])
     query_local = pltpu.make_async_copy(
         q_in.at[:, pl.ds(pl.multiple_of(g * wide, wide), wide)], q_all.at[g], local_sem.at[1]
     )
@@ -295,24 +296,12 @@
 def local(queries, key_states, value_states, key_picks, positions):
     local_rows = queries.shape[0]
     kv_heads = key_states.shape[1] // HD
-    query_heads = queries.shape[1] // HD
 
     angles = positions.astype(jnp.float32)[:, None] * frequency_table(HD)[None, :]
     cosine = jnp.cos(angles)
     sine = jnp.sin(angles)
     cosine = jnp.concatenate([cosine, cosine], axis=1)
     sine = jnp.concatenate([-sine, sine], axis=1)
-
-    sent_kv = pl.pallas_call(
-        lambda *refs: kv_kernel(kv_heads, *refs),
-        out_shape=jax.ShapeDtypeStruct((kv_heads, local_rows, 2 * HD), jnp.bfloat16),
-        name="rope_kv",
-    )(cosine, sine, key_states, value_states)
-    turned_queries = pl.pallas_call(
-        lambda *refs: rope_kernel(query_heads, *refs),
-        out_shape=jax.ShapeDtypeStruct(queries.shape, jnp.bfloat16),
-        name="rope_q",
-    )(cosine, sine, queries)
 
     groups = lax.axis_size("seq")
     all_blocks, picks = key_picks.shape
@@ -358,9 +347,11 @@
     return pl.pallas_call(
         functools.partial(group_kernel, blocks, public, groups // 4),
         out_shape=jax.ShapeDtypeStruct(queries.shape, jnp.bfloat16),
-        in_specs=[smem, smem, smem, vmem, vmem],
+        in_specs=[smem, smem, smem, vmem, vmem, vmem, vmem, anywhere],
         out_specs=anywhere,
         scratch_shapes=[
+            pltpu.VMEM((kv_heads, local_rows, 2 * HD), jnp.bfloat16),
+            pltpu.VMEM(queries.shape, jnp.bfloat16),
             pltpu.VMEM((blocks, SHARE // 2, ROWS, 2 * HD), jnp.bfloat16),
             pltpu.VMEM((blocks, SHARE // 2, ROWS, 2 * HD), jnp.bfloat16),
             pltpu.VMEM((blocks + groups * public, SHARE, ROWS, 2 * HD), jnp.bfloat16),
@@ -373,13 +364,13 @@
             pltpu.SemaphoreType.DMA((kv_heads,)),
             pltpu.SemaphoreType.DMA((30,)),
             pltpu.SemaphoreType.DMA((kv_heads,)),
-            pltpu.SemaphoreType.DMA((5,)),
+            pltpu.SemaphoreType.DMA((6,)),
         ],
         compiler_params=pltpu.CompilerParams(
             collective_id=0, has_side_effects=True, vmem_limit_bytes=48 << 20
         ),
         name="group_attention",
-    )(chosen, held.reshape(-1), bias.reshape(-1), sent_kv, turned_queries)
+    )(chosen, held.reshape(-1), bias.reshape(-1), cosine, sine, key_states, value_states, queries)
 
 
 def solution(mesh):

time: 164 us -> 159 us (0.970)
  Pallas kernels: 157 us -> 152 us
    pallas_call x2 -> x0, Pallas kernels: 4.93 us -> none  [the longest x1 2.84 us: local(): pl.pallas_call(lambda *refs: rope_kernel(query_heads, *refs), out_shape=j...]
    unnamed x9 -> x11, local copies, waits for them, and re-layouts: 3.51 us -> 4.11 us
where the time goes in v4:
time: 159 us; the launch traced here: 158 us
  Pallas kernels  152 us (96%)
  local copies, waits for them, and re-layouts  4.78 us (3%)
    pallas_call x1, Pallas kernels, local(): pl.pallas_call(functools.partial(group_kernel, blocks, public, groups //...  152 us
    unnamed x11, local copies, waits for them, and re-layouts  4.11 us

profile of v4, /device:TPU:1, one launch (start us, length us, event | category | flops | bytes accessed | tf_op | source)
XLA Modules:
  0.0 158.5 jit_solution(168049732593945395)
XLA Ops:
  0.0 0.6 copy-done.4
  0.7 0.7 copy-done.3
  1.3 0.1 or_select_fusion
  1.4 0.1 copy.15
  1.5 0.1 reshape.111.bias_ref
  1.6 0.1 broadcast_compare_fusion
  1.7 0.1 fusion.1
  1.8 0.1 dynamic_slice.9
  1.9 0.1 reshape.112
  2.0 0.2 reduce_window_sum.11
  2.1 0.1 sub.30
  2.3 0.1 dynamic_slice.10
  2.3 0.1 select_reduce_fusion.1.chosen_ref
  2.5 0.2 select_reduce_fusion
  2.7 0.1 copy.14
  2.8 0.1 reshape.110.place_ref
  2.9 0.0 copy-start.2
  2.9 0.3 fusion.2
  3.2 0.1 pad_maximum_fusion
  3.3 0.5 copy-done.1
  3.8 0.1 copy-done.2
  3.9 1.2 copy-done
  5.1 152.4 %group_attention.1 = bf16[128,4096]{1,0:T(8,128)(2,1)S(1)} custom-call(s32[3]{0:T(128)S(1)} %select_reduce_fusion.1.chosen_ref, s32[24]{0:T(128)S(1)} %reshape.110.place_ref, f32[24]{0:T(128)S(1)} %reshape.111.bias_ref, f32[128,128]{1,0:T(8,128)S(1)} %get-tuple-element.10.cos_ref, f32[128,128]{1,0:T(8,128)S(1)} %get-tuple-element.11.sin_ref, ...), custom_call_target="tpu_custom_call" | custom-call | tf_op jit(solution)/shard_map/group_attention/pallas_call | solution.py:347
  157.5 1.0 copy.17
  (12 shorter events, 0.1 us)
Async XLA Ops:
  0.0 0.7 copy-start.4
  0.7 0.7 copy-start.3
  2.9 1.0 copy-start.1
  2.9 1.0 copy-start.2
  3.9 1.2 copy-start

commit v5 on v4

--- a/solution.py
+++ b/solution.py
@@ -173,7 +173,7 @@
         region = own_b.at[away(-j), y_hi]
         arrived(region, fz_sem.at[j])
         send(region, region, fy_sem.at[1, j], y_peer)
-    for j in order:
+    for j in order[::-1]:
         send(
             q_in.at[:, pl.ds(pl.multiple_of(away(j) * wide, wide), wide)],
             q_all.at[g],

time: 159 us -> 159 us (level)
  no operation moved by 1% of the time
where the time goes in v5:
time: 159 us; the launch traced here: 158 us
  Pallas kernels  152 us (96%)
  local copies, waits for them, and re-layouts  4.78 us (3%)
    pallas_call x1, Pallas kernels, local(): pl.pallas_call(functools.partial(group_kernel, blocks, public, groups //...  152 us
    unnamed x11, local copies, waits for them, and re-layouts  4.11 us

profile of v5, /device:TPU:1, one launch (start us, length us, event | category | flops | bytes accessed | tf_op | source)
XLA Modules:
  0.0 158.5 jit_solution(3323852305307042076)
XLA Ops:
  0.0 0.6 copy-done.4
  0.7 0.7 copy-done.3
  1.3 0.1 or_select_fusion
  1.4 0.1 copy.15
  1.5 0.1 reshape.111.bias_ref
  1.6 0.1 broadcast_compare_fusion
  1.7 0.1 fusion.1
  1.8 0.1 dynamic_slice.9
  1.9 0.1 reshape.112
  2.0 0.2 reduce_window_sum.11
  2.1 0.1 sub.30
  2.3 0.1 dynamic_slice.10
  2.3 0.1 select_reduce_fusion.1.chosen_ref
  2.5 0.2 select_reduce_fusion
  2.7 0.1 copy.14
  2.8 0.1 reshape.110.place_ref
  2.9 0.0 copy-start.2
  2.9 0.3 fusion.2
  3.2 0.1 pad_maximum_fusion
  3.3 0.5 copy-done.1
  3.8 0.1 copy-done.2
  3.9 1.2 copy-done
  5.1 152.4 %group_attention.1 = bf16[128,4096]{1,0:T(8,128)(2,1)S(1)} custom-call(s32[3]{0:T(128)S(1)} %select_reduce_fusion.1.chosen_ref, s32[24]{0:T(128)S(1)} %reshape.110.place_ref, f32[24]{0:T(128)S(1)} %reshape.111.bias_ref, f32[128,128]{1,0:T(8,128)S(1)} %get-tuple-element.10.cos_ref, f32[128,128]{1,0:T(8,128)S(1)} %get-tuple-element.11.sin_ref, ...), custom_call_target="tpu_custom_call" | custom-call | tf_op jit(solution)/shard_map/group_attention/pallas_call | solution.py:347
  157.5 1.0 copy.17
  (12 shorter events, 0.1 us)
Async XLA Ops:
  0.0 0.7 copy-start.4
  0.7 0.7 copy-start.3
  2.9 1.0 copy-start.1
  2.9 1.0 copy-start.2
  3.9 1.2 copy-start
